TPU v7x, 32 devices: a whole 2x2x4 slice. The times are simulated.
32 devices in a mesh: section: 2 (over y), row: 16 (over z, x, core).
Axes of the slice: x: 2, y: 2, z: 4, core: 2. Of those that a mesh axis runs over, the one named last changes fastest.
Arguments:
- pair: bfloat16 [2, 128, 128, 128], P(None, 'row'), may hold values from -6 to 6
- valid_tokens: int32 [2], replicated, may hold values from 32 to 128, as said below
- crop_order: int32 [2], replicated, may hold values from 0 to 1, each once
- w_proj: bfloat16 [2, 128, 384], P('section'), may hold values from -0.5 to 0.5
- w_out: bfloat16 [2, 64, 128], P('section'), may hold values from -0.75 to 0.75
- w_in: bfloat16 [2, 128, 1024], P('section'), may hold values from -0.5 to 0.5
- w_back: bfloat16 [2, 512, 128], P('section'), may hold values from -0.25 to 0.25
Outputs:
- final_pair: bfloat16 [2, 128, 128, 128], P('section', 'row')
Inputs may be any that keep to these rules, and one draw needn't show every extreme that they name: `valid_tokens`: valid tokens of each crop; some crop is full and some other has 32. `crop_order`: each crop is taken at exactly one slot.
All inputs are finite; a program needn't handle non-finite values.
Results may differ from a plain program's by a relative error of at most 0.015.
Values may be sent and summed in bfloat16 or wider, within the bound.
No kernel may reach another device: no remote copies, remote signals or barrier semaphores. Data moves between devices by JAX's collectives and lax.ppermute only.
A program may use at most 64 MiB of HBM per device.

v0:
```python
import jax
import jax.numpy as jnp
from jax import lax
from jax.sharding import PartitionSpec as P


def layer_norm(value):
    mean = jnp.mean(value, -1, keepdims=True)
    centred = value - mean
    var = jnp.mean(centred * centred, -1, keepdims=True)
    return centred * lax.rsqrt(var + 1e-05)


def pair_block(state, valid, row_start, w_proj, w_out, w_in, w_back):
    rows_here = state.shape[0]
    count = state.shape[1]
    width = state.shape[2]
    inner = w_out.shape[0]
    trans = w_back.shape[0]
    normed = (
        layer_norm(state.astype(jnp.float32)).astype(jnp.bfloat16).reshape(rows_here * count, width)
    )
    proj = jnp.dot(normed, w_proj, preferred_element_type=jnp.float32).reshape(rows_here, count, -1)
    keep_cols = (jnp.arange(count) < valid).astype(jnp.float32)
    keep_rows = (row_start + jnp.arange(rows_here) < valid).astype(jnp.float32)
    mask = keep_rows[:, None, None] * keep_cols[None, :, None]
    left = (mask * jax.nn.sigmoid(proj[..., inner : 2 * inner]) * proj[..., :inner]).astype(
        jnp.bfloat16
    )
    right = (
        mask * jax.nn.sigmoid(proj[..., 3 * inner : 4 * inner]) * proj[..., 2 * inner : 3 * inner]
    ).astype(jnp.bfloat16)
    gate = jax.nn.sigmoid(proj[..., 4 * inner :])
    left_whole, right_whole = (
        lax.all_to_all(left, "row", split_axis=2, concat_axis=0, tiled=True),
        lax.all_to_all(right, "row", split_axis=2, concat_axis=0, tiled=True),
    )
    tri_part = jnp.einsum(
        "ikc,jkc->ijc", left_whole, right_whole, preferred_element_type=jnp.float32
    )
    tri = lax.all_to_all(
        tri_part.astype(jnp.bfloat16), "row", split_axis=0, concat_axis=2, tiled=True
    ).astype(tri_part.dtype)
    tri_normed = layer_norm(tri).astype(jnp.bfloat16).reshape(rows_here * count, inner)
    update = jnp.dot(tri_normed, w_out, preferred_element_type=jnp.float32).reshape(
        rows_here, count, width
    )
    first = (state.astype(jnp.float32) + gate * update).astype(jnp.bfloat16)
    second = (
        layer_norm(first.astype(jnp.float32)).astype(jnp.bfloat16).reshape(rows_here * count, width)
    )
    hidden = jnp.dot(second, w_in, preferred_element_type=jnp.float32)
    act = (jax.nn.silu(hidden[:, :trans]) * hidden[:, trans:]).astype(jnp.bfloat16)
    back = jnp.dot(act, w_back, preferred_element_type=jnp.float32).reshape(rows_here, count, width)
    return (first.astype(jnp.float32) + back).astype(jnp.bfloat16)


def on_device(pair, valid_tokens, crop_order, w_proj, w_out, w_in, w_back):
    crops = pair.shape[0]
    rows_here = pair.shape[1]
    row_start = lax.axis_index("row") * rows_here
    sections = lax.axis_size("section")
    section = lax.axis_index("section")
    share = crops // sections
    all_proj, all_out, all_in, all_back = (
        lax.all_gather(w_proj, "section", axis=0, tiled=True),
        lax.all_gather(w_out, "section", axis=0, tiled=True),
        lax.all_gather(w_in, "section", axis=0, tiled=True),
        lax.all_gather(w_back, "section", axis=0, tiled=True),
    )
    blocks = all_proj.shape[0]

    def one_crop(index, outputs):
        crop = crop_order[section * share + index]
        valid = valid_tokens[crop]
        state = lax.dynamic_index_in_dim(pair, crop, 0, keepdims=False)

        def apply_block(block, value):
            return pair_block(
                value,
                valid,
                row_start,
                all_proj[block],
                all_out[block],
                all_in[block],
                all_back[block],
            )

        final = lax.fori_loop(0, blocks, apply_block, state)
        return lax.dynamic_update_index_in_dim(outputs, final, index, 0)

    empty = jnp.zeros((share,) + pair.shape[1:], jnp.bfloat16)
    return lax.fori_loop(0, share, one_crop, empty)


def solution(mesh):
    in_specs = (
        P(None, "row", None, None),
        P(),
        P(),
        P("section", None, None),
        P("section", None, None),
        P("section", None, None),
        P("section", None, None),
    )
    out_specs = P("section", "row", None, None)
    return jax.shard_map(
        on_device, mesh=mesh, in_specs=in_specs, out_specs=out_specs, check_vma=False
    )
```

profile of v0, /device:TPU:0, one launch (start us, length us, event | category | flops | bytes accessed | tf_op | source)
XLA Modules:
  0.0 133.9 jit_solution(968022301504030877)
XLA Ops:
  0.0 1.3 dynamic_slice.41
  3.3 1.2 dynamic_slice.43
  4.5 13.2 %all_gather.14 = bf16[2,128,1024]{2,1,0:T(8,128)(2,1)} all-gather(bf16[1,128,1024]{2,1,0:T(8,128)(2,1)} %param.14), channel_id=1, replica_groups=mesh['section'=2,'row'=16] {'section'}, dimensions={0}, use_global_device_ids=true | all-gather | bytes 786432 | tf_op jit(solution)/shard_map/all_gather | solution.py:68
  17.7 5.9 %all_gather.15 = bf16[2,512,128]{2,1,0:T(8,128)(2,1)} all-gather(bf16[1,512,128]{2,1,0:T(8,128)(2,1)} %param.15), channel_id=1, replica_groups=mesh['section'=2,'row'=16] {'section'}, dimensions={0}, use_global_device_ids=true | all-gather | bytes 393216 | tf_op jit(solution)/shard_map/all_gather | solution.py:69
  23.6 5.5 %all_gather.12 = bf16[2,128,384]{2,1,0:T(8,128)(2,1)S(1)} all-gather(bf16[1,128,384]{2,1,0:T(8,128)(2,1)} %param.12), channel_id=1, replica_groups=mesh['section'=2,'row'=16] {'section'}, dimensions={0}, use_global_device_ids=true | all-gather | bytes 294912 | tf_op jit(solution)/shard_map/all_gather | solution.py:66
  29.1 4.6 %all_gather.13 = bf16[2,64,128]{2,1,0:T(8,128)(2,1)S(1)} all-gather(bf16[1,64,128]{2,1,0:T(8,128)(2,1)} %param.13), channel_id=1, replica_groups=mesh['section'=2,'row'=16] {'section'}, dimensions={0}, use_global_device_ids=true | all-gather | bytes 49152 | tf_op jit(solution)/shard_map/all_gather | solution.py:67
  33.7 99.5 %while.21 = (s32[]{:T(128)}, bf16[8,128,128]{2,1,0:T(8,128)(2,1)S(1)}, bf16[2,128,384]{2,1,0:T(8,128)(2,1)S(1)}, s32[]{:T(128)}, s32[]{:T(128)}, /*index=5*/bf16...) while((s32[]{:T(128)}, ...), condition=%wide.region_7.8_spmd, body=%wide.region_0.7_spmd.sunk | while | flops 545067264 | bytes 30512496 | solution.py:89
  34.4 0.5 fusion.73
  34.9 1.4 %fusion.74 = (f32[8,128,64]{2,1,0:T(8,128)}, f32[8,128,64]{2,1,0:T(8,128)S(1)}, f32[8,128,64]{2,1,0:T(8,128)}, f32[8,128,64]{2,1,0:T(8,128)S(1)}) fusion(f32[8,128,384]{2,1,0:T(8,128)S(1)} %fusion.73), kind=kLoop, calls=%fused_computation.62.clone.1 | loop fusion | bytes 2097152 | tf_op jit(solution)/shard_map/while/body/eval_jaxpr/while/body/eval_jaxpr/slice | solution.py:31
  36.2 1.9 %copy.84 = f32[8,128,64]{1,2,0:T(8,128)} copy(f32[8,128,64]{2,1,0:T(8,128)} %get-tuple-element.272) | data formatting | bytes 524288 | tf_op jit(solution)/shard_map/while/body/eval_jaxpr/while
  38.2 1.9 %copy.85 = f32[8,128,64]{1,2,0:T(8,128)} copy(f32[8,128,64]{2,1,0:T(8,128)} %get-tuple-element.273) | data formatting | bytes 524288 | tf_op jit(solution)/shard_map/while/body/eval_jaxpr/while
  40.1 0.9 copy.86
  41.2 0.5 compare_convert_fusion.4
  41.8 0.5 compare_convert_fusion.5
  42.4 1.3 multiply_convert_fusion.5
  43.6 0.7 copy.88
  44.4 5.9 %all-to-all-start = ((bf16[8,128,64]{1,0,2:T(8,128)(2,1)}), bf16[8,128,64]{1,0,2:T(8,128)(2,1)S(1)}, u32[]{:S(2)}, u32[]{:S(2)}) async-start(bf16[8,128,64]{1,0,2:T(8,128)(2,1)} %copy.88), calls=%async_computation | async-start | bytes 262144 | tf_op jit(solution)/shard_map/while/body/eval_jaxpr/while/body/eval_jaxpr/all_to_all | solution.py:35
  50.4 7.8 %all-to-all-done = bf16[8,128,64]{1,0,2:T(8,128)(2,1)S(1)} async-done(((bf16[8,128,64]{1,0,2:T(8,128)(2,1)}), bf16[8,128,64]{1,0,2:T(8,128)(2,1)S(1)}, u32[]{:S(2)}, u32[]{:S(2)}) %all-to-all-start) | async-done | bytes 131104 | tf_op jit(solution)/shard_map/while/body/eval_jaxpr/while/body/eval_jaxpr/all_to_all | solution.py:35
  58.2 10.5 %all_to_all.88 = bf16[8,128,64]{1,0,2:T(8,128)(2,1)S(1)} all-to-all(bf16[8,128,64]{1,0,2:T(8,128)(2,1)S(1)} %copy.89), channel_id=1, replica_groups=mesh['section'=2,'row'=16] {'row'}, dimensions={2} | all-to-all | bytes 262144 | tf_op jit(solution)/shard_map/while/body/eval_jaxpr/while/body/eval_jaxpr/all_to_all | solution.py:36
  68.9 0.8 copy.90
  69.7 3.5 %all-to-all-start.2 = ((bf16[128,128,4]{1,2,0:T(4,128)(2,1)}), bf16[128,128,4]{1,2,0:T(4,128)(2,1)S(1)}, u32[]{:S(2)}, u32[]{:S(2)}) async-start(bf16[128,128,4]{1,2,0:T(4,128)(2,1)} %copy.90), calls=%async_computation.2 | async-start | bytes 262144 | tf_op jit(solution)/shard_map/while/body/eval_jaxpr/while/body/eval_jaxpr/all_to_all | solution.py:41
  73.2 7.9 %all-to-all-done.2 = bf16[128,128,4]{1,2,0:T(4,128)(2,1)S(1)} async-done(((bf16[128,128,4]{1,2,0:T(4,128)(2,1)}), bf16[128,128,4]{1,2,0:T(4,128)(2,1)S(1)}, u32[]{:S(2)}, u32[]{:S(2)}) %all-to-all-start.2) | async-done | bytes 131104 | tf_op jit(solution)/shard_map/while/body/eval_jaxpr/while/body/eval_jaxpr/all_to_all | solution.py:41
  81.3 0.4 fusion.79
  81.8 0.4 multiply_reduce_fusion.2
  82.5 0.7 fusion.80
  83.3 0.7 fusion.81
  84.2 0.4 fusion.82
  85.3 0.5 fusion.73
  85.8 1.4 %fusion.74 = (f32[8,128,64]{2,1,0:T(8,128)}, f32[8,128,64]{2,1,0:T(8,128)S(1)}, f32[8,128,64]{2,1,0:T(8,128)}, f32[8,128,64]{2,1,0:T(8,128)S(1)}) fusion(f32[8,128,384]{2,1,0:T(8,128)S(1)} %fusion.73), kind=kLoop, calls=%fused_computation.62.clone.1 | loop fusion | bytes 2097152 | tf_op jit(solution)/shard_map/while/body/eval_jaxpr/while/body/eval_jaxpr/slice | solution.py:31
  87.2 1.9 %copy.84 = f32[8,128,64]{1,2,0:T(8,128)} copy(f32[8,128,64]{2,1,0:T(8,128)} %get-tuple-element.272) | data formatting | bytes 524288 | tf_op jit(solution)/shard_map/while/body/eval_jaxpr/while
  89.1 1.9 %copy.85 = f32[8,128,64]{1,2,0:T(8,128)} copy(f32[8,128,64]{2,1,0:T(8,128)} %get-tuple-element.273) | data formatting | bytes 524288 | tf_op jit(solution)/shard_map/while/body/eval_jaxpr/while
  91.1 0.9 copy.86
  92.2 0.5 compare_convert_fusion.4
  92.7 0.5 compare_convert_fusion.5
  93.3 1.3 multiply_convert_fusion.5
  94.6 0.7 copy.88
  95.3 3.5 %all-to-all-start = ((bf16[8,128,64]{1,0,2:T(8,128)(2,1)}), bf16[8,128,64]{1,0,2:T(8,128)(2,1)S(1)}, u32[]{:S(2)}, u32[]{:S(2)}) async-start(bf16[8,128,64]{1,0,2:T(8,128)(2,1)} %copy.88), calls=%async_computation | async-start | bytes 262144 | tf_op jit(solution)/shard_map/while/body/eval_jaxpr/while/body/eval_jaxpr/all_to_all | solution.py:35
  99.0 7.8 %all-to-all-done = bf16[8,128,64]{1,0,2:T(8,128)(2,1)S(1)} async-done(((bf16[8,128,64]{1,0,2:T(8,128)(2,1)}), bf16[8,128,64]{1,0,2:T(8,128)(2,1)S(1)}, u32[]{:S(2)}, u32[]{:S(2)}) %all-to-all-start) | async-done | bytes 131104 | tf_op jit(solution)/shard_map/while/body/eval_jaxpr/while/body/eval_jaxpr/all_to_all | solution.py:35
  106.7 10.5 %all_to_all.88 = bf16[8,128,64]{1,0,2:T(8,128)(2,1)S(1)} all-to-all(bf16[8,128,64]{1,0,2:T(8,128)(2,1)S(1)} %copy.89), channel_id=1, replica_groups=mesh['section'=2,'row'=16] {'row'}, dimensions={2} | all-to-all | bytes 262144 | tf_op jit(solution)/shard_map/while/body/eval_jaxpr/while/body/eval_jaxpr/all_to_all | solution.py:36
  117.4 0.8 copy.90
  118.2 3.5 %all-to-all-start.2 = ((bf16[128,128,4]{1,2,0:T(4,128)(2,1)}), bf16[128,128,4]{1,2,0:T(4,128)(2,1)S(1)}, u32[]{:S(2)}, u32[]{:S(2)}) async-start(bf16[128,128,4]{1,2,0:T(4,128)(2,1)} %copy.90), calls=%async_computation.2 | async-start | bytes 262144 | tf_op jit(solution)/shard_map/while/body/eval_jaxpr/while/body/eval_jaxpr/all_to_all | solution.py:41
  121.7 7.9 %all-to-all-done.2 = bf16[128,128,4]{1,2,0:T(4,128)(2,1)S(1)} async-done(((bf16[128,128,4]{1,2,0:T(4,128)(2,1)}), bf16[128,128,4]{1,2,0:T(4,128)(2,1)S(1)}, u32[]{:S(2)}, u32[]{:S(2)}) %all-to-all-start.2) | async-done | bytes 131104 | tf_op jit(solution)/shard_map/while/body/eval_jaxpr/while/body/eval_jaxpr/all_to_all | solution.py:41
  129.9 0.4 fusion.79
  130.3 0.4 multiply_reduce_fusion.2
  131.0 0.7 fusion.80
  131.8 0.7 fusion.81
  132.7 0.4 fusion.82
  133.2 0.7 copy-done.1
  (54 shorter events, 4.0 us)
Async XLA Ops:
  0.0 3.2 %copy-start = (bf16[2,8,128,128]{3,2,1,0:T(8,128)(2,1)S(1)}, bf16[2,8,128,128]{3,2,1,0:T(8,128)(2,1)}, u32[]{:S(2)}) copy-start(bf16[2,8,128,128]{3,2,1,0:T(8,128)(2,1)} %param.9) | copy-start | bytes 1572868
  33.7 0.7 copy-start.4
  44.4 13.8 %all-to-all-start = ((bf16[8,128,64]{1,0,2:T(8,128)(2,1)}), bf16[8,128,64]{1,0,2:T(8,128)(2,1)S(1)}, u32[]{:S(2)}, u32[]{:S(2)}) async-start(bf16[8,128,64]{1,0,2:T(8,128)(2,1)} %copy.88), calls=%async_computation | async-start | bytes 262144 | tf_op jit(solution)/shard_map/while/body/eval_jaxpr/while/body/eval_jaxpr/all_to_all | solution.py:35
  69.7 11.4 %all-to-all-start.2 = ((bf16[128,128,4]{1,2,0:T(4,128)(2,1)}), bf16[128,128,4]{1,2,0:T(4,128)(2,1)S(1)}, u32[]{:S(2)}, u32[]{:S(2)}) async-start(bf16[128,128,4]{1,2,0:T(4,128)(2,1)} %copy.90), calls=%async_computation.2 | async-start | bytes 262144 | tf_op jit(solution)/shard_map/while/body/eval_jaxpr/while/body/eval_jaxpr/all_to_all | solution.py:41
  81.3 1.2 copy-start.2
  83.2 1.0 copy-start.3
  83.2 1.4 %copy-start.5 = (bf16[2,128,384]{2,1,0:T(8,128)(2,1)S(1)}, bf16[2,128,384]{2,1,0:T(8,128)(2,1)}, u32[]{:S(2)}) copy-start(bf16[2,128,384]{2,1,0:T(8,128)(2,1)} %copy-done.4) | copy-start | bytes 589828 | tf_op jit(solution)/shard_map/while/body/eval_jaxpr/while
  84.7 0.7 copy-start.4
  95.3 11.4 %all-to-all-start = ((bf16[8,128,64]{1,0,2:T(8,128)(2,1)}), bf16[8,128,64]{1,0,2:T(8,128)(2,1)S(1)}, u32[]{:S(2)}, u32[]{:S(2)}) async-start(bf16[8,128,64]{1,0,2:T(8,128)(2,1)} %copy.88), calls=%async_computation | async-start | bytes 262144 | tf_op jit(solution)/shard_map/while/body/eval_jaxpr/while/body/eval_jaxpr/all_to_all | solution.py:35
  118.2 11.4 %all-to-all-start.2 = ((bf16[128,128,4]{1,2,0:T(4,128)(2,1)}), bf16[128,128,4]{1,2,0:T(4,128)(2,1)S(1)}, u32[]{:S(2)}, u32[]{:S(2)}) async-start(bf16[128,128,4]{1,2,0:T(4,128)(2,1)} %copy.90), calls=%async_computation.2 | async-start | bytes 262144 | tf_op jit(solution)/shard_map/while/body/eval_jaxpr/while/body/eval_jaxpr/all_to_all | solution.py:41
  129.8 1.2 copy-start.2
  131.8 1.0 copy-start.3
  131.8 1.4 %copy-start.5 = (bf16[2,128,384]{2,1,0:T(8,128)(2,1)S(1)}, bf16[2,128,384]{2,1,0:T(8,128)(2,1)}, u32[]{:S(2)}) copy-start(bf16[2,128,384]{2,1,0:T(8,128)(2,1)} %copy-done.4) | copy-start | bytes 589828 | tf_op jit(solution)/shard_map/while/body/eval_jaxpr/while
  133.2 0.7 copy-start.1
where the time goes:
time: 135 us; the launch traced here: 134 us
  blocking collectives  50.2 us (37%)
  waiting for transfers between devices  31.3 us (23%)
  local copies, waits for them, and re-layouts  19.9 us (15%)
  starting transfers between devices  16.4 us (12%)
  other arithmetic  9.13 us (7%)
  matrix products  4.56 us (3%)
  between operations  1.98 us (1%)
    all_to_all x2, blocking collectives, pair_block(): lax.all_to_all(right, 'row', split_axis=2, concat_axis=0, tiled=True)  21 us
    all_to_all x2, waiting for transfers between devices, pair_block(): lax.all_to_all(tri_part.astype(jnp.bfloat16), 'row', split_axis=0, concat...  15.7 us
    all_to_all x2, waiting for transfers between devices, pair_block(): lax.all_to_all(left, 'row', split_axis=2, concat_axis=0, tiled=True)  15.6 us
    all_gather x1, blocking collectives, on_device(): lax.all_gather(w_in, 'section', axis=0, tiled=True)  13.2 us
    while x24, local copies, waits for them, and re-layouts  10.6 us
    all_to_all x2, starting transfers between devices, pair_block(): lax.all_to_all(left, 'row', split_axis=2, concat_axis=0, tiled=True)  9.42 us
    all_to_all x2, starting transfers between devices, pair_block(): lax.all_to_all(tri_part.astype(jnp.bfloat16), 'row', split_axis=0, concat...  7.03 us
    all_gather x1, blocking collectives, on_device(): lax.all_gather(w_back, 'section', axis=0, tiled=True)  5.94 us
  transfers between devices with their start and end apart: 4, of which 4 were waited for; matrix products, arithmetic and copies ran while one was open for 0% of the time, Pallas kernels for 0%

commit v1 on v0

--- a/solution.py
+++ b/solution.py
@@ -2,6 +2,18 @@
 import jax.numpy as jnp
 from jax import lax
 from jax.sharding import PartitionSpec as P
+
+
+def doubled_up(shard, axis, dim):
+    ways, here, step = (lax.axis_size(axis), lax.axis_index(axis), shard.shape[dim])
+    line, have = (shard, 1)
+    while have < ways:
+        line = jnp.concatenate(
+            [line, lax.ppermute(line, axis, [(d, (d - have) % ways) for d in range(ways)])],
+            axis=dim,
+        )
+        have = 2 * have
+    return jnp.roll(line, here * step, axis=dim)
 
 
 def layer_norm(value):
@@ -65,7 +77,7 @@
     all_proj, all_out, all_in, all_back = (
         lax.all_gather(w_proj, "section", axis=0, tiled=True),
         lax.all_gather(w_out, "section", axis=0, tiled=True),
-        lax.all_gather(w_in, "section", axis=0, tiled=True),
+        doubled_up(w_in, "section", 0),
         lax.all_gather(w_back, "section", axis=0, tiled=True),
     )
     blocks = all_proj.shape[0]

time: 135 us -> 127 us (0.941)
  blocking collectives: 50.2 us -> 37 us
  starting transfers between devices: 16.4 us -> 19.4 us
  other arithmetic: 9.13 us -> 11.2 us
    all_gather x1 -> x0, blocking collectives: 13.2 us -> none  [on_device(): lax.all_gather(w_in, 'section', axis=0, tiled=True)]
    ppermute x0 -> x1, starting transfers between devices: none -> 3 us  [doubled_up(): lax.ppermute(line, axis, [(d, (d - have) % ways) for d in range(ways)])]
    concatenate x0 -> x1, other arithmetic: none -> 2.12 us  [doubled_up(): return jnp.roll(line, here * step, axis=dim)]
  transfers between devices with their start and end apart: 4 -> 5, of which waited for: 4 -> 4; matrix products, arithmetic and copies ran while one was open for 0% -> 2% of each run, Pallas kernels for 0% -> 0%
where the time goes in v1:
time: 127 us; the launch traced here: 126 us
  blocking collectives  37 us (29%)
  waiting for transfers between devices  31.3 us (25%)
  local copies, waits for them, and re-layouts  19.8 us (16%)
  starting transfers between devices  19.4 us (15%)
  other arithmetic  11.2 us (9%)
  matrix products  4.57 us (4%)
  between operations  1.99 us (2%)
    all_to_all x2, blocking collectives, pair_block(): lax.all_to_all(right, 'row', split_axis=2, concat_axis=0, tiled=True)  21 us
    all_to_all x2, waiting for transfers between devices, pair_block(): lax.all_to_all(tri_part.astype(jnp.bfloat16), 'row', split_axis=0, concat...  15.7 us
    all_to_all x2, waiting for transfers between devices, pair_block(): lax.all_to_all(left, 'row', split_axis=2, concat_axis=0, tiled=True)  15.6 us
    while x24, local copies, waits for them, and re-layouts  10.6 us
    all_to_all x2, starting transfers between devices, pair_block(): lax.all_to_all(left, 'row', split_axis=2, concat_axis=0, tiled=True)  9.42 us
    all_to_all x2, starting transfers between devices, pair_block(): lax.all_to_all(tri_part.astype(jnp.bfloat16), 'row', split_axis=0, concat...  7.03 us
    all_gather x1, blocking collectives, on_device(): lax.all_gather(w_back, 'section', axis=0, tiled=True)  5.94 us
    all_gather x1, blocking collectives, on_device(): lax.all_gather(w_proj, 'section', axis=0, tiled=True)  5.48 us
  transfers between devices with their start and end apart: 5, of which 4 were waited for; matrix products, arithmetic and copies ran while one was open for 2% of the time, Pallas kernels for 0%

profile of v1, /device:TPU:0, one launch (start us, length us, event | category | flops | bytes accessed | tf_op | source)
XLA Modules:
  0.0 125.8 jit_solution(17041446096462136765)
XLA Ops:
  0.0 3.0 %collective-permute-start = (bf16[1,128,1024]{2,1,0:T(8,128)(2,1)}, bf16[1,128,1024]{2,1,0:T(8,128)(2,1)S(1)}, u32[]{:S(2)}, u32[]{:S(2)}) collective-permute-start(bf16[1,128,1024]{2,1,0:T(8,128)(2,1)} %param.14), channel_id=1, source_target_pairs={{0,16},{16,0},{1,17},{17,1},{2,18},{18,2},{3,19},{19,3},{4,20},{20... | collective-permute-start | bytes 786440 | tf_op jit(solution)/shard_map/ppermute | solution.py:12
  3.0 1.2 dynamic_slice.45
  6.2 1.2 dynamic_slice.47
  7.4 4.6 %all_gather.10 = bf16[2,64,128]{2,1,0:T(8,128)(2,1)S(1)} all-gather(bf16[1,64,128]{2,1,0:T(8,128)(2,1)} %param.13), channel_id=1, replica_groups=mesh['section'=2,'row'=16] {'section'}, dimensions={0}, use_global_device_ids=true | all-gather | bytes 49152 | tf_op jit(solution)/shard_map/all_gather | solution.py:79
  12.0 5.5 %all_gather.9 = bf16[2,128,384]{2,1,0:T(8,128)(2,1)S(1)} all-gather(bf16[1,128,384]{2,1,0:T(8,128)(2,1)} %param.12), channel_id=1, replica_groups=mesh['section'=2,'row'=16] {'section'}, dimensions={0}, use_global_device_ids=true | all-gather | bytes 294912 | tf_op jit(solution)/shard_map/all_gather | solution.py:78
  17.5 5.9 %all_gather.11 = bf16[2,512,128]{2,1,0:T(8,128)(2,1)} all-gather(bf16[1,512,128]{2,1,0:T(8,128)(2,1)} %param.15), channel_id=1, replica_groups=mesh['section'=2,'row'=16] {'section'}, dimensions={0}, use_global_device_ids=true | all-gather | bytes 393216 | tf_op jit(solution)/shard_map/all_gather | solution.py:81
  23.5 2.1 %fusion.43 = bf16[2,128,1024]{2,1,0:T(8,128)(2,1)} fusion(s32[]{:T(128)S(6)} %select_n.37, bf16[1,128,1024]{2,1,0:T(8,128)(2,1)} %param.14, bf16[1,128,1024]{2,1,0:T(8,128)(2,1)S(1)} %collective-permute-done), kind=kLoop, calls=%fused_computation.67 | loop fusion | flops 786432 | bytes 1048580 | tf_op jit(solution)/shard_map/jit(_roll_dynamic)/concatenate | solution.py:16
  25.6 99.5 %while.21 = (s32[]{:T(128)}, bf16[8,128,128]{2,1,0:T(8,128)(2,1)S(1)}, bf16[2,128,384]{2,1,0:T(8,128)(2,1)S(1)}, s32[]{:T(128)}, s32[]{:T(128)}, /*index=5*/bf16...) while((s32[]{:T(128)}, ...), condition=%wide.region_7.8_spmd, body=%wide.region_0.7_spmd.sunk | while | flops 545067264 | bytes 30512496 | solution.py:101
  26.3 0.5 fusion.76
  26.8 1.4 %fusion.77 = (f32[8,128,64]{2,1,0:T(8,128)}, f32[8,128,64]{2,1,0:T(8,128)S(1)}, f32[8,128,64]{2,1,0:T(8,128)}, f32[8,128,64]{2,1,0:T(8,128)S(1)}) fusion(f32[8,128,384]{2,1,0:T(8,128)S(1)} %fusion.76), kind=kLoop, calls=%fused_computation.69.clone.1 | loop fusion | bytes 2097152 | tf_op jit(solution)/shard_map/while/body/eval_jaxpr/while/body/eval_jaxpr/slice | solution.py:43
  28.1 1.9 %copy.84 = f32[8,128,64]{1,2,0:T(8,128)} copy(f32[8,128,64]{2,1,0:T(8,128)} %get-tuple-element.272) | data formatting | bytes 524288 | tf_op jit(solution)/shard_map/while/body/eval_jaxpr/while
  30.1 1.9 %copy.85 = f32[8,128,64]{1,2,0:T(8,128)} copy(f32[8,128,64]{2,1,0:T(8,128)} %get-tuple-element.273) | data formatting | bytes 524288 | tf_op jit(solution)/shard_map/while/body/eval_jaxpr/while
  32.0 0.9 copy.86
  33.1 0.5 compare_convert_fusion.4
  33.6 0.5 compare_convert_fusion.5
  34.3 1.3 multiply_convert_fusion.5
  35.5 0.7 copy.88
  36.3 5.9 %all-to-all-start = ((bf16[8,128,64]{1,0,2:T(8,128)(2,1)}), bf16[8,128,64]{1,0,2:T(8,128)(2,1)S(1)}, u32[]{:S(2)}, u32[]{:S(2)}) async-start(bf16[8,128,64]{1,0,2:T(8,128)(2,1)} %copy.88), calls=%async_computation | async-start | bytes 262144 | tf_op jit(solution)/shard_map/while/body/eval_jaxpr/while/body/eval_jaxpr/all_to_all | solution.py:47
  42.3 7.8 %all-to-all-done = bf16[8,128,64]{1,0,2:T(8,128)(2,1)S(1)} async-done(((bf16[8,128,64]{1,0,2:T(8,128)(2,1)}), bf16[8,128,64]{1,0,2:T(8,128)(2,1)S(1)}, u32[]{:S(2)}, u32[]{:S(2)}) %all-to-all-start) | async-done | bytes 131104 | tf_op jit(solution)/shard_map/while/body/eval_jaxpr/while/body/eval_jaxpr/all_to_all | solution.py:47
  50.1 10.5 %all_to_all.88 = bf16[8,128,64]{1,0,2:T(8,128)(2,1)S(1)} all-to-all(bf16[8,128,64]{1,0,2:T(8,128)(2,1)S(1)} %copy.89), channel_id=1, replica_groups=mesh['section'=2,'row'=16] {'row'}, dimensions={2} | all-to-all | bytes 262144 | tf_op jit(solution)/shard_map/while/body/eval_jaxpr/while/body/eval_jaxpr/all_to_all | solution.py:48
  60.8 0.8 copy.90
  61.6 3.5 %all-to-all-start.2 = ((bf16[128,128,4]{1,2,0:T(4,128)(2,1)}), bf16[128,128,4]{1,2,0:T(4,128)(2,1)S(1)}, u32[]{:S(2)}, u32[]{:S(2)}) async-start(bf16[128,128,4]{1,2,0:T(4,128)(2,1)} %copy.90), calls=%async_computation.2 | async-start | bytes 262144 | tf_op jit(solution)/shard_map/while/body/eval_jaxpr/while/body/eval_jaxpr/all_to_all | solution.py:53
  65.1 7.9 %all-to-all-done.2 = bf16[128,128,4]{1,2,0:T(4,128)(2,1)S(1)} async-done(((bf16[128,128,4]{1,2,0:T(4,128)(2,1)}), bf16[128,128,4]{1,2,0:T(4,128)(2,1)S(1)}, u32[]{:S(2)}, u32[]{:S(2)}) %all-to-all-start.2) | async-done | bytes 131104 | tf_op jit(solution)/shard_map/while/body/eval_jaxpr/while/body/eval_jaxpr/all_to_all | solution.py:53
  73.2 0.4 fusion.82
  73.7 0.4 multiply_reduce_fusion.2
  74.4 0.7 fusion.83
  75.1 0.7 fusion.84
  76.1 0.4 fusion.85
  77.2 0.5 fusion.76
  77.7 1.4 %fusion.77 = (f32[8,128,64]{2,1,0:T(8,128)}, f32[8,128,64]{2,1,0:T(8,128)S(1)}, f32[8,128,64]{2,1,0:T(8,128)}, f32[8,128,64]{2,1,0:T(8,128)S(1)}) fusion(f32[8,128,384]{2,1,0:T(8,128)S(1)} %fusion.76), kind=kLoop, calls=%fused_computation.69.clone.1 | loop fusion | bytes 2097152 | tf_op jit(solution)/shard_map/while/body/eval_jaxpr/while/body/eval_jaxpr/slice | solution.py:43
  79.1 1.9 %copy.84 = f32[8,128,64]{1,2,0:T(8,128)} copy(f32[8,128,64]{2,1,0:T(8,128)} %get-tuple-element.272) | data formatting | bytes 524288 | tf_op jit(solution)/shard_map/while/body/eval_jaxpr/while
  81.0 1.9 %copy.85 = f32[8,128,64]{1,2,0:T(8,128)} copy(f32[8,128,64]{2,1,0:T(8,128)} %get-tuple-element.273) | data formatting | bytes 524288 | tf_op jit(solution)/shard_map/while/body/eval_jaxpr/while
  83.0 0.9 copy.86
  84.0 0.5 compare_convert_fusion.4
  84.6 0.5 compare_convert_fusion.5
  85.2 1.3 multiply_convert_fusion.5
  86.5 0.7 copy.88
  87.2 3.5 %all-to-all-start = ((bf16[8,128,64]{1,0,2:T(8,128)(2,1)}), bf16[8,128,64]{1,0,2:T(8,128)(2,1)S(1)}, u32[]{:S(2)}, u32[]{:S(2)}) async-start(bf16[8,128,64]{1,0,2:T(8,128)(2,1)} %copy.88), calls=%async_computation | async-start | bytes 262144 | tf_op jit(solution)/shard_map/while/body/eval_jaxpr/while/body/eval_jaxpr/all_to_all | solution.py:47
  90.8 7.8 %all-to-all-done = bf16[8,128,64]{1,0,2:T(8,128)(2,1)S(1)} async-done(((bf16[8,128,64]{1,0,2:T(8,128)(2,1)}), bf16[8,128,64]{1,0,2:T(8,128)(2,1)S(1)}, u32[]{:S(2)}, u32[]{:S(2)}) %all-to-all-start) | async-done | bytes 131104 | tf_op jit(solution)/shard_map/while/body/eval_jaxpr/while/body/eval_jaxpr/all_to_all | solution.py:47
  98.6 10.5 %all_to_all.88 = bf16[8,128,64]{1,0,2:T(8,128)(2,1)S(1)} all-to-all(bf16[8,128,64]{1,0,2:T(8,128)(2,1)S(1)} %copy.89), channel_id=1, replica_groups=mesh['section'=2,'row'=16] {'row'}, dimensions={2} | all-to-all | bytes 262144 | tf_op jit(solution)/shard_map/while/body/eval_jaxpr/while/body/eval_jaxpr/all_to_all | solution.py:48
  109.3 0.8 copy.90
  110.1 3.5 %all-to-all-start.2 = ((bf16[128,128,4]{1,2,0:T(4,128)(2,1)}), bf16[128,128,4]{1,2,0:T(4,128)(2,1)S(1)}, u32[]{:S(2)}, u32[]{:S(2)}) async-start(bf16[128,128,4]{1,2,0:T(4,128)(2,1)} %copy.90), calls=%async_computation.2 | async-start | bytes 262144 | tf_op jit(solution)/shard_map/while/body/eval_jaxpr/while/body/eval_jaxpr/all_to_all | solution.py:53
  113.6 7.9 %all-to-all-done.2 = bf16[128,128,4]{1,2,0:T(4,128)(2,1)S(1)} async-done(((bf16[128,128,4]{1,2,0:T(4,128)(2,1)}), bf16[128,128,4]{1,2,0:T(4,128)(2,1)S(1)}, u32[]{:S(2)}, u32[]{:S(2)}) %all-to-all-start.2) | async-done | bytes 131104 | tf_op jit(solution)/shard_map/while/body/eval_jaxpr/while/body/eval_jaxpr/all_to_all | solution.py:53
  121.7 0.4 fusion.82
  122.9 0.7 fusion.83
  123.7 0.7 fusion.84
  124.6 0.4 fusion.85
  125.1 0.7 copy-done.1
  (56 shorter events, 4.4 us)
Async XLA Ops:
  0.0 23.4 %copy-start = (bf16[2,8,128,128]{3,2,1,0:T(8,128)(2,1)S(1)}, bf16[2,8,128,128]{3,2,1,0:T(8,128)(2,1)}, u32[]{:S(2)}) copy-start(bf16[2,8,128,128]{3,2,1,0:T(8,128)(2,1)} %param.9) | copy-start | bytes 1572868
  0.0 23.5 %collective-permute-start = (bf16[1,128,1024]{2,1,0:T(8,128)(2,1)}, bf16[1,128,1024]{2,1,0:T(8,128)(2,1)S(1)}, u32[]{:S(2)}, u32[]{:S(2)}) collective-permute-start(bf16[1,128,1024]{2,1,0:T(8,128)(2,1)} %param.14), channel_id=1, source_target_pairs={{0,16},{16,0},{1,17},{17,1},{2,18},{18,2},{3,19},{19,3},{4,20},{20... | collective-permute-start | bytes 786440 | tf_op jit(solution)/shard_map/ppermute | solution.py:12
  25.6 0.7 copy-start.4
  36.3 13.8 %all-to-all-start = ((bf16[8,128,64]{1,0,2:T(8,128)(2,1)}), bf16[8,128,64]{1,0,2:T(8,128)(2,1)S(1)}, u32[]{:S(2)}, u32[]{:S(2)}) async-start(bf16[8,128,64]{1,0,2:T(8,128)(2,1)} %copy.88), calls=%async_computation | async-start | bytes 262144 | tf_op jit(solution)/shard_map/while/body/eval_jaxpr/while/body/eval_jaxpr/all_to_all | solution.py:47
  61.6 11.4 %all-to-all-start.2 = ((bf16[128,128,4]{1,2,0:T(4,128)(2,1)}), bf16[128,128,4]{1,2,0:T(4,128)(2,1)S(1)}, u32[]{:S(2)}, u32[]{:S(2)}) async-start(bf16[128,128,4]{1,2,0:T(4,128)(2,1)} %copy.90), calls=%async_computation.2 | async-start | bytes 262144 | tf_op jit(solution)/shard_map/while/body/eval_jaxpr/while/body/eval_jaxpr/all_to_all | solution.py:53
  73.2 1.2 copy-start.2
  75.1 1.0 copy-start.3
  75.1 1.4 %copy-start.5 = (bf16[2,128,384]{2,1,0:T(8,128)(2,1)S(1)}, bf16[2,128,384]{2,1,0:T(8,128)(2,1)}, u32[]{:S(2)}) copy-start(bf16[2,128,384]{2,1,0:T(8,128)(2,1)} %copy-done.4) | copy-start | bytes 589828 | tf_op jit(solution)/shard_map/while/body/eval_jaxpr/while
  76.5 0.7 copy-start.4
  87.2 11.4 %all-to-all-start = ((bf16[8,128,64]{1,0,2:T(8,128)(2,1)}), bf16[8,128,64]{1,0,2:T(8,128)(2,1)S(1)}, u32[]{:S(2)}, u32[]{:S(2)}) async-start(bf16[8,128,64]{1,0,2:T(8,128)(2,1)} %copy.88), calls=%async_computation | async-start | bytes 262144 | tf_op jit(solution)/shard_map/while/body/eval_jaxpr/while/body/eval_jaxpr/all_to_all | solution.py:47
  110.1 11.4 %all-to-all-start.2 = ((bf16[128,128,4]{1,2,0:T(4,128)(2,1)}), bf16[128,128,4]{1,2,0:T(4,128)(2,1)S(1)}, u32[]{:S(2)}, u32[]{:S(2)}) async-start(bf16[128,128,4]{1,2,0:T(4,128)(2,1)} %copy.90), calls=%async_computation.2 | async-start | bytes 262144 | tf_op jit(solution)/shard_map/while/body/eval_jaxpr/while/body/eval_jaxpr/all_to_all | solution.py:53
  121.7 1.2 copy-start.2
  123.6 1.0 copy-start.3
  123.7 1.4 %copy-start.5 = (bf16[2,128,384]{2,1,0:T(8,128)(2,1)S(1)}, bf16[2,128,384]{2,1,0:T(8,128)(2,1)}, u32[]{:S(2)}) copy-start(bf16[2,128,384]{2,1,0:T(8,128)(2,1)} %copy-done.4) | copy-start | bytes 589828 | tf_op jit(solution)/shard_map/while/body/eval_jaxpr/while
  125.1 0.7 copy-start.1
